TPU v7x, 256 devices: a whole 4x4x8 slice. The times are simulated.
256 devices in a mesh: rows: 8 (over y, core), labels: 32 (over x, z).
Axes of the slice: x: 4, y: 4, z: 8, core: 2. Of those that a mesh axis runs over, the one named last changes fastest.
Arguments:
- embeddings: bfloat16 [8192, 768], P(('rows', 'labels')), may hold values from -6 to 6
- class_weight: bfloat16 [65536, 768], P('labels'), may hold values from -0.4375 to 0.4375
- class_bias: float32 [65536], P('labels'), may hold values from -10 to -8
- propensity: float32 [65536], P('labels'), may hold values from 0.1 to 0.9
- label_ids: int32 [8192, 32], P('rows'), may hold values from 0 to 65535
- label_count: int32 [8192], P('rows'), may hold values from 1 to 32
- label_bins: int32 [65536], P('labels'), may hold values from 0 to 15
- prior_mean: float32 [16], replicated, may hold values from 0.1 to 0.9
Outputs:
- new_propensity: float32 [65536], P('labels')
- weight_grad: bfloat16 [65536, 768], P('labels', 'rows')
- embed_grad: bfloat16 [8192, 768], P(('rows', 'labels'))
Inputs may be any that keep to these rules, and one draw needn't show every extreme that they name: `label_ids`: entries past a row's count are padding and are ignored; ids may repeat.
All inputs are finite; a program needn't handle non-finite values.
Results may differ from a plain program's by a relative error of at most 0.014.
Values may be sent and summed in bfloat16 or wider, within the bound.
No kernel may reach another device: no remote copies, remote signals or barrier semaphores. Data moves between devices by JAX's collectives and lax.ppermute only.
A program may use at most 64 MiB of HBM per device.

v0:
```python
import jax
import jax.numpy as jnp
from jax import lax
from jax.sharding import PartitionSpec as P


def dense_observed(label_ids, label_count, offset, width):
    slots = jnp.arange(label_ids.shape[1], dtype=jnp.int32)
    local = label_ids - offset
    valid = (slots[None, :] < label_count[:, None]) & (local >= 0) & (local < width)
    column = jnp.where(valid, local, width)
    lanes = jnp.arange(width, dtype=jnp.int32)
    hits = column[:, :, None] == lanes[None, None, :]
    return jnp.max(hits.astype(jnp.float32), axis=1)


def bin_prior(bins, prior_mean):
    levels = jnp.arange(prior_mean.shape[0], dtype=jnp.int32)
    onehot = (bins[:, None] == levels[None, :]).astype(jnp.float32)
    return jnp.sum(onehot * prior_mean[None, :], axis=1)


def body(
    embeddings, class_weight, class_bias, propensity, label_ids, label_count, label_bins, prior_mean
):
    width = class_weight.shape[0]
    gathered = lax.all_gather(embeddings, "labels", axis=0, tiled=True)
    offset = lax.axis_index("labels") * width
    scores = (
        lax.dot_general(
            gathered, class_weight, (((1,), (1,)), ((), ())), preferred_element_type=jnp.float32
        )
        + class_bias[None, :]
    )
    prob = jax.nn.sigmoid(scores)
    observed = dense_observed(label_ids, label_count, offset, width)
    posterior = observed + (1.0 - observed) * prob * (1.0 - propensity[None, :]) / (
        1.0 - prob * propensity[None, :]
    )
    local_post = jnp.sum(posterior, axis=0)
    local_obs = jnp.sum(observed, axis=0)
    post_sum, obs_sum = lax.psum((local_post, local_obs), "rows")
    updated = (obs_sum + 8.0 * bin_prior(label_bins, prior_mean)) / (post_sum + 8.0)
    residual_grad = (prob - posterior).astype(jnp.bfloat16)
    weight_terms = lax.dot_general(
        residual_grad, gathered, (((0,), (0,)), ((), ())), preferred_element_type=jnp.float32
    )
    weight_summed = lax.psum_scatter(
        weight_terms.astype(jnp.bfloat16), "rows", scatter_dimension=1, tiled=True
    ).astype(jnp.float32)
    weight_grad = (weight_summed / updated[:, None]).astype(jnp.bfloat16)
    scaled_weight = (class_weight.astype(jnp.float32) / updated[:, None]).astype(jnp.bfloat16)
    embed_terms = jnp.dot(residual_grad, scaled_weight, preferred_element_type=jnp.float32)
    embed_total = lax.psum_scatter(
        embed_terms.astype(jnp.bfloat16), "labels", scatter_dimension=0, tiled=True
    )
    return (updated, weight_grad, embed_total)


def solution(mesh):
    placed = (
        P(("rows", "labels"), None),
        P("labels", None),
        P("labels"),
        P("labels"),
        P("rows", None),
        P("rows"),
        P("labels"),
        P(),
    )
    return jax.shard_map(
        body,
        mesh=mesh,
        in_specs=placed,
        out_specs=(P("labels"), P("labels", "rows"), P(("rows", "labels"), None)),
        check_vma=False,
    )
```

profile of v0, /device:TPU:16, one launch (start us, length us, event | category | flops | bytes accessed | tf_op | source)
XLA Modules:
  0.0 372.5 jit_solution(14143030236094921360)
XLA Ops:
  7.2 0.0 copy-start.1
  7.2 0.0 copy-start.6
  7.2 0.0 all-gather.2.cloned.1.call-start
  7.2 0.7 all-gather.2.cloned.1.call-update
  7.9 0.0 reduce-scatter.3.cloned.1.call-start
  8.0 0.9 fusion.5
  8.9 0.2 copy.12
  9.1 0.7 broadcast_subtract_fusion
  9.8 51.6 %convert_reduce_fusion = f32[1024,2048]{1,0:T(8,128)} fusion(s32[1024,32]{1,0:T(8,128)S(1)} %copy.12), kind=kLoop, calls=%fused_computation | loop fusion | flops 199229440 | bytes 8519680 | tf_op jit(solution)/shard_map/reduce_max | solution.py:14
  61.5 28.8 %all-gather.2.cloned.1.call-done = bf16[1024,768]{1,0:T(8,128)(2,1)} async-done(((bf16[32,768]{1,0:T(8,128)(2,1)}), bf16[1024,768]{1,0:T(8,128)(2,1)}) %all-gather.2.cloned.1.call-update) | async-done | bytes 1572880 | tf_op jit(solution)/shard_map/all_gather | solution.py:27
  90.3 0.0 copy-done.1
  90.3 0.0 copy-done.6
  90.3 0.0 copy-start.5
  90.3 10.4 %fusion.6 = (f32[2048]{0:T(1024)S(1)}, f32[2048]{0:T(1024)S(1)}, bf16[1024,2048]{1,0:T(8,128)(2,1)S(1)}) fusion(f32[1024,2048]{1,0:T(8,128)} %convert_reduce_fusion, f32[2048]{0:T(1024)S(1)} %copy-done.1, f32[2048]{0:T(1024)S(1)} %broadcast_subtract_fusion, f32[2048]{0:T(1024)S(1)} %copy-done.6, bf16[1024,768]{1,0:T(8,128)(2,1)} %all-gather.2.cloned.1.call-done, ...), kind=kOutput, calls=%fused_computation.19 | convolution fusion | flops 3252678656 | bytes 17342464 | tf_op jit(solution)/shard_map/dot_general | solution.py:30
  100.7 0.0 copy-start.7
  100.7 1.9 copy-done.7
  102.6 0.0 copy-done.5
  102.6 0.0 copy-start.2
  102.6 0.0 copy-start.3
  102.6 0.0 copy-start.4
  102.7 5.0 %convolution_convert_fusion = bf16[2048,768]{0,1:T(8,128)(2,1)} fusion(bf16[1024,2048]{1,0:T(8,128)(2,1)S(1)} %get-tuple-element.7, bf16[1024,768]{1,0:T(8,128)(2,1)S(1)} %copy-done.5), kind=kOutput, calls=%fused_computation.6 | convolution fusion | flops 3222798336 | bytes 8912896 | tf_op jit(solution)/shard_map/dot_general | solution.py:45
  107.7 0.0 reduce-scatter.3.cloned.1.call-update
  107.7 0.0 reduce-scatter.5.cloned.1.call-start
  107.8 0.0 copy-done.2
  107.8 0.0 copy-done.3
  107.8 0.1 select_reduce_fusion
  107.9 19.3 %all-reduce = (f32[2048]{0:T(1024)S(1)}, f32[2048]{0:T(1024)S(1)}) all-reduce(f32[2048]{0:T(1024)S(1)} %get-tuple-element.4, f32[2048]{0:T(1024)S(1)} %get-tuple-element.3), channel_id=1, replica_groups=mesh['rows'=8,'labels'=32] {'rows'}, use_global_device_ids=true, to_apply=%region_5.6 | all-reduce | flops 4096 | bytes 32768 | tf_op jit(solution)/shard_map/psum | solution.py:42
  127.2 0.0 copy-done.4
  127.2 0.0 copy-start
  127.3 7.0 %fusion.1 = bf16[1024,768]{1,0:T(8,128)(2,1)} fusion(bf16[1024,2048]{1,0:T(8,128)(2,1)} %copy-done.7, bf16[2048,768]{1,0:T(8,128)(2,1)S(1)} %copy-done.4, f32[2048]{0:T(1024)S(1)} %add_divide_fusion.1), kind=kOutput, calls=%fused_computation.8 | convolution fusion | flops 3226730496 | bytes 8921088 | tf_op jit(solution)/shard_map/dot_general | solution.py:53
  134.3 0.0 reduce-scatter.5.cloned.1.call-update
  134.3 4.8 %reduce-scatter.3.cloned.1.call-done = bf16[2048,96]{0,1:T(8,128)(2,1)} async-done(((bf16[2048,768]{0,1:T(8,128)(2,1)}), bf16[2048,96]{0,1:T(8,128)(2,1)}) %reduce-scatter.3.cloned.1.call-update) | async-done | bytes 393232 | tf_op jit(solution)/shard_map/reduce_scatter | solution.py:48
  139.1 0.0 copy-done
  139.1 1.8 divide_convert_fusion.4
  140.9 225.0 %reduce-scatter.5.cloned.1.call-done = bf16[32,768]{1,0:T(8,128)(2,1)} async-done(((bf16[1024,768]{1,0:T(8,128)(2,1)}), bf16[32,768]{1,0:T(8,128)(2,1)}) %reduce-scatter.5.cloned.1.call-update) | async-done | bytes 49168 | tf_op jit(solution)/shard_map/reduce_scatter | solution.py:54
  (1 shorter events, 0.0 us)
Async XLA Ops:
  7.2 83.1 %copy-start.1 = (f32[2048]{0:T(1024)S(1)}, f32[2048]{0:T(1024)}, u32[]{:S(2)}) copy-start(f32[2048]{0:T(1024)} %param.11) | copy-start | bytes 24580
  7.2 83.1 %copy-start.6 = (f32[2048]{0:T(1024)S(1)}, f32[2048]{0:T(1024)}, u32[]{:S(2)}) copy-start(f32[2048]{0:T(1024)} %param.10) | copy-start | bytes 24580
  7.2 83.1 %all-gather.2.cloned.1.call-start = ((), (), s32[]{:S(2)}) async-start(), calls=%async_computation.2 | async-start | bytes 1622016 | tf_op jit(solution)/shard_map/all_gather | solution.py:27
  7.9 131.2 %reduce-scatter.3.cloned.1.call-start = ((), (), s32[]{:S(2)}) async-start(), calls=%async_computation.3 | async-start | bytes 3538944 | tf_op jit(solution)/shard_map/reduce_scatter | solution.py:48
  90.3 12.3 %copy-start.5 = (bf16[1024,768]{1,0:T(8,128)(2,1)S(1)}, bf16[1024,768]{1,0:T(8,128)(2,1)}, u32[]{:S(2)}) copy-start(bf16[1024,768]{1,0:T(8,128)(2,1)} %all-gather.2.cloned.1.call-done) | copy-start | bytes 4718596
  100.7 1.9 copy-start.7
  102.6 5.1 %copy-start.2 = (s32[2048]{0:T(1024)S(1)}, s32[2048]{0:T(1024)}, u32[]{:S(2)}) copy-start(s32[2048]{0:T(1024)} %param.14) | copy-start | bytes 24580
  102.6 5.1 %copy-start.3 = (f32[16]{0:T(128)S(1)}, f32[16]{0:T(128)}, u32[]{:S(2)}) copy-start(f32[16]{0:T(128)} %param.15) | copy-start | bytes 196
  102.6 24.6 %copy-start.4 = (bf16[2048,768]{1,0:T(8,128)(2,1)S(1)}, bf16[2048,768]{1,0:T(8,128)(2,1)}, u32[]{:S(2)}) copy-start(bf16[2048,768]{1,0:T(8,128)(2,1)} %param.9) | copy-start | bytes 9437188
  107.7 258.2 %reduce-scatter.5.cloned.1.call-start = ((), (), s32[]{:S(2)}) async-start(), calls=%async_computation.4 | async-start | bytes 1622016 | tf_op jit(solution)/shard_map/reduce_scatter | solution.py:54
  127.2 11.9 %copy-start = (f32[2048]{0:T(1024)}, f32[2048]{0:T(1024)S(1)}, u32[]{:S(2)}) copy-start(f32[2048]{0:T(1024)S(1)} %add_divide_fusion.1) | copy-start | bytes 24580
Sparse Core Ops, SparseCore 0:
  10.6 79.6 all-gather.1
  107.8 31.2 reduce-scatter.2
  143.5 222.3 reduce-scatter.4
where the time goes:
time: 373 us; the launch traced here: 372 us
  waiting for transfers between devices  259 us (69%)
  other arithmetic  55.2 us (15%)
  matrix products  22.4 us (6%)
  blocking collectives  19.3 us (5%)
  between operations  13.8 us (4%)
    reduce_scatter x1, waiting for transfers between devices, body(): lax.psum_scatter(embed_terms.astype(jnp.bfloat16), 'labels', scatter_dime...  225 us
    reduce_max x1, other arithmetic, dense_observed(): return jnp.max(hits.astype(jnp.float32), axis=1)  51.6 us
    all_gather x1, waiting for transfers between devices, body(): gathered = lax.all_gather(embeddings, 'labels', axis=0, tiled=True)  28.8 us
    psum x1, blocking collectives, body(): post_sum, obs_sum = lax.psum((local_post, local_obs), 'rows')  19.3 us
    dot_general x1, matrix products, body(): lax.dot_general(gathered, class_weight, (((1,), (1,)), ((), ())), preferr...  10.4 us
  transfers between devices with their start and end apart: 3, of which 3 were waited for; matrix products, arithmetic and copies ran while one was open for 17% of the time, Pallas kernels for 0%

commit v1 on v0

--- a/solution.py
+++ b/solution.py
@@ -24,7 +24,10 @@
     embeddings, class_weight, class_bias, propensity, label_ids, label_count, label_bins, prior_mean
 ):
     width = class_weight.shape[0]
-    gathered = lax.all_gather(embeddings, "labels", axis=0, tiled=True)
+    devices = lax.axis_size("labels")
+    tiles = jnp.stack([embeddings for _ in range(devices)])
+    tiles = lax.all_to_all(tiles, "labels", split_axis=0, concat_axis=0)
+    gathered = jnp.concatenate(tiles, axis=0)
     offset = lax.axis_index("labels") * width
     scores = (
         lax.dot_general(

time: 373 us -> 361 us (0.968)
  waiting for transfers between devices: 259 us -> 232 us
  starting transfers between devices: 0.12 us -> 11.5 us
    all_gather x1 -> x0, waiting for transfers between devices: 28.8 us -> none  [body(): gathered = lax.all_gather(embeddings, 'labels', axis=0, tiled=True)]
    all_to_all x0 -> x1, starting transfers between devices: none -> 11.4 us  [body(): tiles = lax.all_to_all(tiles, 'labels', split_axis=0, concat_axis=0)]
  transfers between devices with their start and end apart: 3 -> 3, of which waited for: 3 -> 2; matrix products, arithmetic and copies ran while one was open for 17% -> 18% of each run, Pallas kernels for 0% -> 0%
where the time goes in v1:
time: 361 us; the launch traced here: 360 us
  waiting for transfers between devices  232 us (64%)
  other arithmetic  55.2 us (15%)
  matrix products  23.2 us (6%)
  blocking collectives  19.7 us (5%)
  between operations  14.1 us (4%)
  starting transfers between devices  11.5 us (3%)
  local copies, waits for them, and re-layouts  4.35 us (1%)
    reduce_scatter x1, waiting for transfers between devices, body(): lax.psum_scatter(embed_terms.astype(jnp.bfloat16), 'labels', scatter_dime...  225 us
    reduce_max x1, other arithmetic, dense_observed(): return jnp.max(hits.astype(jnp.float32), axis=1)  51.6 us
    psum x1, blocking collectives, body(): post_sum, obs_sum = lax.psum((local_post, local_obs), 'rows')  19.7 us
    all_to_all x1, starting transfers between devices, body(): tiles = lax.all_to_all(tiles, 'labels', split_axis=0, concat_axis=0)  11.4 us
    dot_general x1, matrix products, body(): lax.dot_general(gathered, class_weight, (((1,), (1,)), ((), ())), preferr...  10.1 us
    dot_general x1, matrix products, body(): jnp.dot(residual_grad, scaled_weight, preferred_element_type=jnp.float32)  8.08 us
  transfers between devices with their start and end apart: 3, of which 2 were waited for; matrix products, arithmetic and copies ran while one was open for 18% of the time, Pallas kernels for 0%

profile of v1, /device:TPU:16, one launch (start us, length us, event | category | flops | bytes accessed | tf_op | source)
XLA Modules:
  0.0 360.3 jit_solution(7804694392445038440)
XLA Ops:
  7.2 2.2 stack.2
  9.4 0.0 copy-start.1
  9.4 0.0 copy-start.4
  9.4 11.4 %all-to-all-start = ((bf16[32,32,768]{2,1,0:T(8,128)(2,1)}), bf16[32,32,768]{2,1,0:T(8,128)(2,1)S(1)}, u32[]{:S(2)}, u32[]{:S(2)}) async-start(bf16[32,32,768]{2,1,0:T(8,128)(2,1)} %stack.2), calls=%async_computation | async-start | bytes 3145728 | tf_op jit(solution)/shard_map/all_to_all | solution.py:29
  20.8 0.0 reduce-scatter.3.cloned.1.call-start
  20.9 0.9 fusion.5
  21.8 0.2 copy.12
  22.0 0.7 broadcast_subtract_fusion
  22.7 51.6 %convert_reduce_fusion = f32[1024,2048]{1,0:T(8,128)} fusion(s32[1024,32]{1,0:T(8,128)S(1)} %copy.12), kind=kLoop, calls=%fused_computation | loop fusion | flops 199229440 | bytes 8519680 | tf_op jit(solution)/shard_map/reduce_max | solution.py:14
  74.4 0.0 all-to-all-done
  74.4 0.0 copy-done.1
  74.4 0.0 copy-done.4
  74.4 10.1 %fusion.6 = (f32[2048]{0:T(1024)S(1)}, f32[2048]{0:T(1024)S(1)}, bf16[1024,2048]{1,0:T(8,128)(2,1)S(1)}) fusion(f32[1024,2048]{1,0:T(8,128)} %convert_reduce_fusion, f32[2048]{0:T(1024)S(1)} %copy-done.1, f32[2048]{0:T(1024)S(1)} %broadcast_subtract_fusion, f32[2048]{0:T(1024)S(1)} %copy-done.4, bf16[1024,768]{1,0:T(8,128)(2,1)S(1)} %bitcast.6, ...), kind=kOutput, calls=%fused_computation.19 | convolution fusion | flops 3252678656 | bytes 17342464 | tf_op jit(solution)/shard_map/dot_general | solution.py:33
  84.5 0.0 copy-start.5
  84.5 1.9 copy-done.5
  86.4 0.0 copy-start.2
  86.4 0.0 copy-start.3
  86.4 5.0 %convolution_convert_fusion = bf16[2048,768]{0,1:T(8,128)(2,1)} fusion(bf16[1024,2048]{1,0:T(8,128)(2,1)S(1)} %get-tuple-element.7, bf16[1024,768]{1,0:T(8,128)(2,1)S(1)} %bitcast.7), kind=kOutput, calls=%fused_computation.6 | convolution fusion | flops 3222798336 | bytes 8912896 | tf_op jit(solution)/shard_map/dot_general | solution.py:48
  91.5 0.0 reduce-scatter.3.cloned.1.call-update
  91.5 0.0 reduce-scatter.5.cloned.1.call-start
  91.5 0.0 copy-done.2
  91.5 0.0 copy-done.3
  91.6 0.1 select_reduce_fusion
  91.7 19.7 %all-reduce = (f32[2048]{0:T(1024)S(1)}, f32[2048]{0:T(1024)S(1)}) all-reduce(f32[2048]{0:T(1024)S(1)} %get-tuple-element.4, f32[2048]{0:T(1024)S(1)} %get-tuple-element.3), channel_id=1, replica_groups=mesh['rows'=8,'labels'=32] {'rows'}, use_global_device_ids=true, to_apply=%region_5.6 | all-reduce | flops 4096 | bytes 32768 | tf_op jit(solution)/shard_map/psum | solution.py:45
  111.4 0.0 copy-start
  111.4 8.1 %fusion.1 = bf16[1024,768]{1,0:T(8,128)(2,1)} fusion(bf16[1024,2048]{1,0:T(8,128)(2,1)} %copy-done.5, bf16[2048,768]{1,0:T(8,128)(2,1)} %param.9, f32[2048]{0:T(1024)S(1)} %add_divide_fusion.1), kind=kOutput, calls=%fused_computation.8 | convolution fusion | flops 3226730496 | bytes 8921088 | tf_op jit(solution)/shard_map/dot_general | solution.py:56
  119.4 0.0 reduce-scatter.5.cloned.1.call-update
  119.5 7.0 %reduce-scatter.3.cloned.1.call-done = bf16[2048,96]{0,1:T(8,128)(2,1)} async-done(((bf16[2048,768]{0,1:T(8,128)(2,1)}), bf16[2048,96]{0,1:T(8,128)(2,1)}) %reduce-scatter.3.cloned.1.call-update) | async-done | bytes 393232 | tf_op jit(solution)/shard_map/reduce_scatter | solution.py:51
  126.5 0.0 copy-done
  126.5 1.8 divide_convert_fusion.4
  128.3 225.1 %reduce-scatter.5.cloned.1.call-done = bf16[32,768]{1,0:T(8,128)(2,1)} async-done(((bf16[1024,768]{1,0:T(8,128)(2,1)}), bf16[32,768]{1,0:T(8,128)(2,1)}) %reduce-scatter.5.cloned.1.call-update) | async-done | bytes 49168 | tf_op jit(solution)/shard_map/reduce_scatter | solution.py:57
  (1 shorter events, 0.0 us)
Async XLA Ops:
  9.4 65.0 %copy-start.1 = (f32[2048]{0:T(1024)S(1)}, f32[2048]{0:T(1024)}, u32[]{:S(2)}) copy-start(f32[2048]{0:T(1024)} %param.11) | copy-start | bytes 24580
  9.4 65.0 %copy-start.4 = (f32[2048]{0:T(1024)S(1)}, f32[2048]{0:T(1024)}, u32[]{:S(2)}) copy-start(f32[2048]{0:T(1024)} %param.10) | copy-start | bytes 24580
  9.4 65.0 %all-to-all-start = ((bf16[32,32,768]{2,1,0:T(8,128)(2,1)}), bf16[32,32,768]{2,1,0:T(8,128)(2,1)S(1)}, u32[]{:S(2)}, u32[]{:S(2)}) async-start(bf16[32,32,768]{2,1,0:T(8,128)(2,1)} %stack.2), calls=%async_computation | async-start | bytes 3145728 | tf_op jit(solution)/shard_map/all_to_all | solution.py:29
  20.8 105.7 %reduce-scatter.3.cloned.1.call-start = ((), (), s32[]{:S(2)}) async-start(), calls=%async_computation.3 | async-start | bytes 3538944 | tf_op jit(solution)/shard_map/reduce_scatter | solution.py:51
  84.5 1.9 copy-start.5
  86.4 5.1 %copy-start.2 = (s32[2048]{0:T(1024)S(1)}, s32[2048]{0:T(1024)}, u32[]{:S(2)}) copy-start(s32[2048]{0:T(1024)} %param.14) | copy-start | bytes 24580
  86.4 5.1 %copy-start.3 = (f32[16]{0:T(128)S(1)}, f32[16]{0:T(128)}, u32[]{:S(2)}) copy-start(f32[16]{0:T(128)} %param.15) | copy-start | bytes 196
  91.5 262.0 %reduce-scatter.5.cloned.1.call-start = ((), (), s32[]{:S(2)}) async-start(), calls=%async_computation.4 | async-start | bytes 1622016 | tf_op jit(solution)/shard_map/reduce_scatter | solution.py:57
  111.4 15.2 %copy-start = (f32[2048]{0:T(1024)}, f32[2048]{0:T(1024)S(1)}, u32[]{:S(2)}) copy-start(f32[2048]{0:T(1024)S(1)} %add_divide_fusion.1) | copy-start | bytes 24580
Sparse Core Ops, SparseCore 0:
  91.6 34.8 reduce-scatter.2
  130.9 222.4 reduce-scatter.4
